TPU v7x, 256 devices: a whole 4x4x8 slice. The times are simulated.
256 devices in a mesh: order: 32 (over x, y, core), axial: 8 (over z).
Axes of the slice: x: 4, y: 4, z: 8, core: 2. Of those that a mesh axis runs over, the one named last changes fastest.
Arguments:
- coefficients: bfloat16 [4, 2, 1024, 16, 1024], P(None, None, 'order', 'axial'), may hold values from -0.005859375 to 0.005859375
- order_lists: int32 [1024], replicated, may hold values from 0 to 1023, as said below
- lengths: int32 [1024], replicated, may hold values from 128 to 1024, as said below
Outputs:
- advection: bfloat16 [3, 2, 1024, 16, 1024], P(None, None, 'order', 'axial')
Inputs may be any that keep to these rules, and one draw needn't show every extreme that they name: `order_lists`: a permutation of the orders 0 to 1023; the device with index j along order holds slots j * 32 to (j + 1) * 32 - 1 of coefficients and advection. lengths[m] minus (128 + ((1023 - m) * 768) // 1023) lies in 0 to 128.
All inputs are finite; a program needn't handle non-finite values.
Results may differ from a plain program's by a relative error of at most 0.0095.
Values may be sent and summed in bfloat16 or wider, within the bound.
No kernel may reach another device: no remote copies, remote signals or barrier semaphores. Data moves between devices by JAX's collectives and lax.ppermute only.
A program may use at most 128 MiB of HBM per device.

v0:
```python
import functools
import math

import jax
import jax.numpy as jnp
import numpy as np
from jax import lax
from jax.experimental import pallas as pl
from jax.experimental.pallas import tpu as pltpu
from jax.sharding import PartitionSpec as P

R = 1024
F32 = jnp.float32
BF16 = jnp.bfloat16


def radial_constants(radius_count, mode_count):
    radius_ids = np.arange(radius_count)
    mode_ids = np.arange(mode_count)
    phases = mode_ids[None, :] * (2 * radius_ids[:, None] + 1) % (4 * radius_count)
    cosines = np.cos(phases * (math.pi / (2 * radius_count))).astype(np.float32)
    synthesis = cosines.astype(jnp.bfloat16)
    analysis = (cosines * np.float32(math.sqrt(2.0 / radius_count))).astype(jnp.bfloat16)
    return synthesis, analysis


def plane_matrices(slots):
    width = 2 * slots * 2
    pair = width // 2
    inner = np.arange(width)
    plane, rest = inner % 2, inner // 2
    gather = np.zeros((width, width), np.float32)
    gather[inner, plane * pair + rest] = 1.0
    eye = np.eye(pair, dtype=np.float32)
    own = np.kron(eye, np.array([[0, 8], [-8, 0]], np.float32))
    low = np.kron(eye, np.array([[1, -8], [0, 1]], np.float32))
    high = np.kron(eye, np.array([[-1, 0], [8, -1]], np.float32))
    rows = np.concatenate([own, low, high], axis=1)
    swap = np.roll(np.eye(width, dtype=np.float32), pair, axis=1)
    both = np.concatenate([gather, gather @ swap], axis=1)
    slope = rows.T @ both
    return (
        rows.astype(jnp.bfloat16),
        both.astype(jnp.bfloat16),
        slope.astype(jnp.bfloat16),
        gather.T.astype(jnp.bfloat16),
    )


def dot(a, b, dims):
    return lax.dot_general(a, b, (dims, ((), ())), preferred_element_type=F32)


def masked_rows(block, lens, weight):
    modes = lax.broadcasted_iota(jnp.int32, block.shape, 1)
    return jnp.where(modes < lens, block.astype(F32) * weight, 0.0)


def raw_kernel(x_ref, lens_ref, weight_ref, table_ref, out_ref, held):
    @pl.when(pl.program_id(0) == 0)
    def _():
        for start in range(0, x_ref.shape[0], 128):
            part = pl.ds(start, 128)
            held[part, :] = masked_rows(x_ref[part, :], lens_ref[...], weight_ref[...]).astype(BF16)

    out_ref[...] = dot(table_ref[...], held[...], ((1,), (1,))).astype(BF16)


def slope_kernel(x_ref, low_ref, high_ref, lens_ref, weight_ref, rows_ref, table_ref, out_ref, held):
    @pl.when(pl.program_id(0) == 0)
    def _():
        for start in range(0, x_ref.shape[0], 128):
            part = pl.ds(start, 128)
            stacked = jnp.concatenate([x_ref[part, :], low_ref[part, :], high_ref[part, :]], axis=0)
            slope = dot(rows_ref[...], stacked, ((1,), (0,)))
            held[part, :] = masked_rows(slope, lens_ref[...], weight_ref[...]).astype(BF16)

    out_ref[...] = dot(table_ref[...], held[...], ((1,), (1,))).astype(BF16)


def whole(shape):
    return pl.BlockSpec(shape, lambda i: (0,) * len(shape))


def radial_raw(x, lens, weight, table, step=256):
    rows, modes = x.shape
    return pl.pallas_call(
        raw_kernel,
        grid=(R // step,),
        out_shape=jax.ShapeDtypeStruct((R, rows), BF16),
        in_specs=[whole(x.shape), whole(lens.shape), whole(weight.shape),
                  pl.BlockSpec((step, modes), lambda i: (i, 0))],
        out_specs=pl.BlockSpec((step, rows), lambda i: (i, 0)),
        scratch_shapes=[pltpu.VMEM((rows, modes), BF16)],
        compiler_params=pltpu.CompilerParams(vmem_limit_bytes=24 << 20),
        name="radial_raw",
    )(x, lens, weight, table)


def radial_slope(x, low, high, lens, weight, rows_map, table, step=256):
    rows, modes = x.shape
    return pl.pallas_call(
        slope_kernel,
        grid=(R // step,),
        out_shape=jax.ShapeDtypeStruct((R, rows), BF16),
        in_specs=[whole(x.shape), whole(x.shape), whole(x.shape), whole(lens.shape),
                  whole(weight.shape), whole(rows_map.shape),
                  pl.BlockSpec((step, modes), lambda i: (i, 0))],
        out_specs=pl.BlockSpec((step, rows), lambda i: (i, 0)),
        scratch_shapes=[pltpu.VMEM((rows, modes), BF16)],
        compiler_params=pltpu.CompilerParams(vmem_limit_bytes=24 << 20),
        name="radial_slope",
    )(x, low, high, lens, weight, rows_map, table)


def table_kernel(orders_ref, out_ref):
    slots = orders_ref.shape[0]
    points = out_ref.shape[1]
    orders = jnp.broadcast_to(orders_ref[...], (slots, 128))
    lane = lax.broadcasted_iota(jnp.int32, (slots, 128), 1)
    unit = 2.0 * math.pi / points
    fine = ((orders * lane) & (points - 1)).astype(F32) * unit
    turn = ((orders * 128) & (points - 1)).astype(F32) * unit
    cos_now, sin_now = jnp.cos(fine), jnp.sin(fine)
    cos_turn, sin_turn = jnp.cos(turn), jnp.sin(turn)
    for block in range(points // 128):
        part = pl.ds(block * 128, 128)
        out_ref[0:slots, part] = cos_now.astype(BF16)
        out_ref[slots:2 * slots, part] = (-sin_now).astype(BF16)
        cos_now, sin_now = (
            cos_now * cos_turn - sin_now * sin_turn,
            sin_now * cos_turn + cos_now * sin_turn,
        )


def azimuthal_table(orders, groups, slots, points):
    return pl.pallas_call(
        table_kernel,
        grid=(groups,),
        out_shape=jax.ShapeDtypeStruct((groups * 2 * slots, points), BF16),
        in_specs=[pl.BlockSpec((slots, 1), lambda i: (i, 0))],
        out_specs=pl.BlockSpec((2 * slots, points), lambda i: (i, 0)),
        compiler_params=pltpu.CompilerParams(vmem_limit_bytes=24 << 20),
        name="azimuthal_table",
    )(orders)


def physical_kernel(groups, band, scale, raw_ref, slope_ref, low_ref, high_ref, both_ref,
                    dz_ref, table_ref, out_ref, lhs, acc):
    step = pl.program_id(0)
    width = both_ref.shape[0]
    half = width // 2
    low_lanes = lax.broadcasted_iota(jnp.int32, (band, width), 1) < half

    @pl.when(step == 0)
    def _():
        acc[...] = jnp.zeros_like(acc)
        for field in range(4):
            if field < 2:
                mapped = dot(slope_ref[:, field * width:(field + 1) * width], both_ref[...], ((1,), (0,)))
            elif field == 2:
                joined = jnp.concatenate([raw_ref[:, 0:width], low_ref[...], high_ref[...]], axis=1)
                mapped = dot(joined, dz_ref[...], ((1,), (0,)))
            else:
                mapped = dot(raw_ref[:, width:2 * width], both_ref[...], ((1,), (0,)))
            for pair in range(groups // 2):
                even = mapped[2 * pair * band:(2 * pair + 1) * band]
                odd = mapped[(2 * pair + 1) * band:(2 * pair + 2) * band]
                first = jnp.where(low_lanes, even[:, :width], odd[:, width:])
                second = jnp.where(low_lanes, even[:, width:], odd[:, :width])
                cols = pl.ds(pair * width, width)
                lhs[(2 * field) * band:(2 * field + 1) * band, cols] = first.astype(BF16)
                lhs[(2 * field + 1) * band:(2 * field + 2) * band, cols] = second.astype(BF16)

    values = dot(lhs[...], table_ref[...], ((1,), (0,)))
    axial = values[6 * band:8 * band] * (1.0 / 12.0)
    products = jnp.concatenate(
        [(values[2 * g * band:(2 * g + 2) * band] * axial).astype(BF16) for g in range(3)], axis=0
    )
    acc[...] += dot(products, table_ref[...], ((1,), (1,)))

    @pl.when(step == pl.num_programs(0) - 1)
    def _():
        for g in range(3):
            for pair in range(groups // 2):
                cols = pl.ds(pair * width, width)
                first = acc[(2 * g) * band:(2 * g + 1) * band, cols] * scale
                second = acc[(2 * g + 1) * band:(2 * g + 2) * band, cols] * scale
                even = jnp.where(low_lanes, first, pltpu.roll(second, half, 1))
                odd = jnp.where(low_lanes, pltpu.roll(first, half, 1), second)
                out_cols = pl.ds(g * width, width)
                out_ref[2 * pair * band:(2 * pair + 1) * band, out_cols] = even.astype(BF16)
                out_ref[(2 * pair + 1) * band:(2 * pair + 2) * band, out_cols] = odd.astype(BF16)


def physical_stage(raw, slope, low, high, both, dz, table, groups, band, step=512):
    rows, points = table.shape
    width = both.shape[0]
    return pl.pallas_call(
        functools.partial(physical_kernel, groups, band, math.sqrt(2.0 / points)),
        grid=(points // step,),
        out_shape=jax.ShapeDtypeStruct((groups * band, 3 * width), BF16),
        in_specs=[whole(raw.shape), whole(slope.shape), whole(low.shape), whole(high.shape),
                  whole(both.shape), whole(dz.shape),
                  pl.BlockSpec((rows, step), lambda i: (0, i))],
        out_specs=whole((groups * band, 3 * width)),
        scratch_shapes=[pltpu.VMEM((8 * band, rows), BF16), pltpu.VMEM((6 * band, rows), F32)],
        compiler_params=pltpu.CompilerParams(vmem_limit_bytes=40 << 20),
        name="physical_stage",
    )(raw, slope, low, high, both, dz, table)


def final_kernel(x_ref, lens_ref, back_ref, table_ref, out_ref, held):
    width = back_ref.shape[0]
    step = pl.program_id(0)
    columns = table_ref.shape[1]

    @pl.when(step == 0)
    def _():
        for g in range(3):
            part = slice(g * width, (g + 1) * width)
            held[:, part] = dot(x_ref[:, part], back_ref[...], ((1,), (0,))).astype(BF16)

    result = dot(held[...], table_ref[...], ((0,), (0,)))
    modes = lax.broadcasted_iota(jnp.int32, (width, columns), 1) + step * columns
    keep = modes < lens_ref[...]
    for g in range(3):
        out_ref[g * width:(g + 1) * width, :] = jnp.where(
            keep, result[g * width:(g + 1) * width], 0.0
        ).astype(BF16)


def radial_analysis(x, lens, back, table, step=256):
    radii, lanes = x.shape
    modes = table.shape[1]
    return pl.pallas_call(
        final_kernel,
        grid=(modes // step,),
        out_shape=jax.ShapeDtypeStruct((lanes, modes), BF16),
        in_specs=[whole(x.shape), whole(lens.shape), whole(back.shape),
                  pl.BlockSpec((radii, step), lambda i: (0, i))],
        out_specs=pl.BlockSpec((lanes, step), lambda i: (0, i)),
        scratch_shapes=[pltpu.VMEM((radii, lanes), BF16)],
        compiler_params=pltpu.CompilerParams(vmem_limit_bytes=24 << 20),
        name="radial_analysis",
    )(x, lens, back, table)


def shift(block, offset):
    count = lax.axis_size("axial")
    return lax.ppermute(block, "axial", [(i, (i + offset) % count) for i in range(count)])


def exchange(block):
    return lax.all_to_all(block, "order", split_axis=0, concat_axis=0, tiled=True)


def shards(coefficients, order_lists, lengths):
    field_count, part_count, slots, planes, modes = coefficients.shape
    order_count = order_lists.shape[0]
    points = 2 * order_count
    groups = lax.axis_size("order")
    band = R // groups
    width = part_count * slots * planes
    synthesis, analysis = radial_constants(R, modes)
    rows_map, both, dz, back = plane_matrices(slots)

    rows = coefficients.reshape(field_count * width, modes)
    sloped, raw = rows[:2 * width], rows[2 * width:]
    low, high = shift(sloped, 1), shift(sloped, -1)

    owned = lax.dynamic_slice_in_dim(order_lists, lax.axis_index("order") * slots, slots)
    catalog = jnp.arange(order_count, dtype=jnp.int32)
    own_lengths = jnp.sum(
        jnp.where(owned[:, None] == catalog[None, :], lengths[None, :], 0), axis=1
    )
    spread = (part_count, slots, planes)
    lens = jnp.broadcast_to(own_lengths[None, :, None], spread).reshape(width, 1)
    weight = jnp.where(owned == 0, 1.0, 2.0).astype(F32)
    weight = jnp.broadcast_to(weight[None, :, None], spread).reshape(width, 1)

    raw_bands = exchange(radial_raw(raw, lens, weight, synthesis))
    table = azimuthal_table(order_lists.reshape(order_count, 1), groups, slots, points)
    own_band = raw_bands[:, :width]
    low_band, high_band = shift(own_band, 1), shift(own_band, -1)
    slope_bands = exchange(radial_slope(sloped, low, high, lens, weight, rows_map, synthesis))
    spectral = physical_stage(
        raw_bands, slope_bands, low_band, high_band, both, dz, table, groups, band
    )
    result = radial_analysis(exchange(spectral), lens, back, analysis)
    return result.reshape(3, part_count, slots, planes, modes)


def solution(mesh):
    placed = (P(None, None, "order", "axial", None), P(), P())
    return jax.shard_map(
        shards,
        mesh=mesh,
        in_specs=placed,
        out_specs=P(None, None, "order", "axial", None),
        check_vma=False,
    )
```

profile of v0, /device:TPU:1, one launch (start us, length us, event | category | flops | bytes accessed | tf_op | source)
XLA Modules:
  0.0 89.2 jit_solution(13363723371232993960)
XLA Ops:
  0.0 2.9 %fusion = (bf16[2,2,32,2,1024]{4,3,2,1,0:T(2,128)(2,1)S(1)}, bf16[2,2,32,2,1024]{4,3,2,1,0:T(2,128)(2,1)}) fusion(bf16[4,2,32,2,1024]{4,3,2,1,0:T(2,128)(2,1)} %param.9), kind=kLoop, calls=%fused_computation.3 | loop fusion | bytes 2097152 | tf_op jit(solution)/shard_map/slice | solution.py:269
  2.9 0.2 slice.18.x_ref
  3.1 6.5 %collective-permute-start.1 = (bf16[256,1024]{1,0:T(8,128)(2,1)S(1)}, bf16[256,1024]{1,0:T(8,128)(2,1)}, u32[]{:S(2)}, u32[]{:S(2)}) collective-permute-start(bf16[256,1024]{1,0:T(8,128)(2,1)S(1)} %slice.18.x_ref), channel_id=1, source_target_pairs={{0,7},{1,0},{2,1},{3,2},{4,3},{5,4},{6,5},{7,6},{8,15},{9,8},{10,9... | collective-permute-start | bytes 1572872 | tf_op jit(solution)/shard_map/ppermute | solution.py:251
  9.6 0.1 compare_select_fusion
  9.6 0.2 select_reduce_fusion
  9.8 0.1 broadcast_in_dim.37
  9.9 0.1 reshape.29.lens_ref
  10.0 0.1 broadcast_in_dim.40
  10.1 0.1 reshape.30.weight_ref
  10.1 1.2 %slice.16.x_ref = bf16[256,1024]{1,0:T(8,128)(2,1)S(1)} reshape(bf16[2,2,32,2,1024]{4,3,2,1,0:T(2,128)(2,1)} %get-tuple-element.8) | data formatting | bytes 1048576 | tf_op jit(solution)/shard_map/slice | solution.py:269
  11.4 0.0 copy-start.7
  11.4 1.7 %radial_raw.1 = bf16[1024,256]{1,0:T(8,128)(2,1)S(1)} custom-call(bf16[256,1024]{1,0:T(8,128)(2,1)S(1)} %slice.16.x_ref, s32[128,1]{1,0:T(8,128)S(1)} %reshape.29.lens_ref, f32[128,1]{1,0:T(8,128)S(1)} %reshape.30.weight_ref, bf16[1024,1024]{1,0:T(8,128)(2,1)S(1)} %copy-done.2), custom_call_target="tpu_custom_call" | custom-call | tf_op jit(solution)/shard_map/radial_raw/pallas_call | solution.py:87
  13.1 0.0 copy-start.5
  13.1 0.8 copy-done.5
  13.9 8.0 %all-to-all-start = ((bf16[32,32,256]{2,1,0:T(8,128)(2,1)}), bf16[32,32,256]{2,1,0:T(8,128)(2,1)S(1)}, u32[]{:S(2)}, u32[]{:S(2)}) async-start(bf16[32,32,256]{2,1,0:T(8,128)(2,1)} %bitcast.12), calls=%async_computation | async-start | bytes 1048576 | tf_op jit(solution)/shard_map/all_to_all | solution.py:255
  21.9 0.0 collective-permute-done.1.high_ref
  21.9 1.4 %collective-permute-done.low_ref = bf16[256,1024]{1,0:T(8,128)(2,1)} collective-permute-done((bf16[256,1024]{1,0:T(8,128)(2,1)S(1)}, bf16[256,1024]{1,0:T(8,128)(2,1)}, u32[]{:S(2)}, u32[]{:S(2)}) %collective-permute-start) | collective-permute-done | bytes 524320 | tf_op jit(solution)/shard_map/ppermute | solution.py:251
  23.3 3.0 %radial_slope.1 = bf16[1024,256]{1,0:T(8,128)(2,1)S(1)} custom-call(bf16[256,1024]{1,0:T(8,128)(2,1)S(1)} %slice.18.x_ref, bf16[256,1024]{1,0:T(8,128)(2,1)} %collective-permute-done.low_ref, bf16[256,1024]{1,0:T(8,128)(2,1)} %collective-permute-done.1.high_ref, s32[128,1]{1,0:T(8,128)S(1)} %reshape.29.lens_ref, f32[128,1]{1,0:T(8,128)S(1)} %reshape.30.weight_ref, ...), custom_call_target="tpu_custom_call" | custom-call | tf_op jit(solution)/shard_map/radial_slope/pallas_call | solution.py:102
  26.4 0.8 copy-done.4
  27.2 6.3 %all-to-all-done = bf16[32,32,256]{2,1,0:T(8,128)(2,1)S(1)} async-done(((bf16[32,32,256]{2,1,0:T(8,128)(2,1)}), bf16[32,32,256]{2,1,0:T(8,128)(2,1)S(1)}, u32[]{:S(2)}, u32[]{:S(2)}) %all-to-all-start) | async-done | bytes 524320 | tf_op jit(solution)/shard_map/all_to_all | solution.py:255
  33.5 3.7 %all-to-all-start.1 = ((bf16[32,32,256]{2,1,0:T(8,128)(2,1)}), bf16[32,32,256]{2,1,0:T(8,128)(2,1)S(1)}, u32[]{:S(2)}, u32[]{:S(2)}) async-start(bf16[32,32,256]{2,1,0:T(8,128)(2,1)} %bitcast.11), calls=%async_computation.1 | async-start | bytes 1048576 | tf_op jit(solution)/shard_map/all_to_all | solution.py:255
  37.3 3.0 %collective-permute-start.3 = (bf16[1024,128]{1,0:T(8,128)(2,1)S(1)}, bf16[1024,128]{1,0:T(8,128)(2,1)S(1)}, u32[]{:S(2)}, u32[]{:S(2)}) collective-permute-start(bf16[1024,128]{1,0:T(8,128)(2,1)S(1)} %slice.20), channel_id=1, source_target_pairs={{0,7},{1,0},{2,1},{3,2},{4,3},{5,4},{6,5},{7,6},{8,15},{9,8},{10,9... | collective-permute-start | bytes 786440 | tf_op jit(solution)/shard_map/ppermute | solution.py:251
  40.3 0.2 copy.25.orders_ref
  40.5 0.0 copy-start.6
  40.5 0.0 copy-start.8
  40.5 8.9 %azimuthal_table.1.table_ref = bf16[2048,2048]{1,0:T(8,128)(2,1)S(1)} custom-call(s32[1024,1]{1,0:T(8,128)S(1)} %copy.25.orders_ref), custom_call_target="tpu_custom_call" | custom-call | tf_op jit(solution)/shard_map/azimuthal_table/pallas_call | solution.py:137
  49.4 3.2 %copy-done = bf16[2048,2048]{1,0:T(8,128)(2,1)} copy-done((bf16[2048,2048]{1,0:T(8,128)(2,1)}, bf16[2048,2048]{1,0:T(8,128)(2,1)S(1)}, u32[]{:S(2)}) %copy-start) | copy-done | bytes 8388632
  52.7 3.4 %copy-done.1 = bf16[2048,2048]{1,0:T(8,128)(2,1)S(1)} copy-done((bf16[2048,2048]{1,0:T(8,128)(2,1)S(1)}, bf16[2048,2048]{1,0:T(8,128)(2,1)}, u32[]{:S(2)}) %copy-start.1) | copy-done | bytes 8388632
  56.1 7.8 %physical_stage.1 = bf16[1024,384]{1,0:T(8,128)(2,1)S(1)} custom-call(bf16[1024,256]{1,0:T(8,128)(2,1)S(1)} %bitcast.8, bf16[1024,256]{1,0:T(8,128)(2,1)S(1)} %bitcast.13, bf16[1024,128]{1,0:T(8,128)(2,1)S(1)} %collective-permute-done.2.low_ref, bf16[1024,128]{1,0:T(8,128)(2,1)S(1)} %collective-permute-done.3.high_ref, bf16[128,256]{1,0:T(8,128)(2,1)S(1)} %copy-done.8, ...), custom_call_target="tpu_custom_call" | custom-call | tf_op jit(solution)/shard_map/physical_stage/pallas_call | solution.py:199
  63.9 21.6 %all_to_all.33 = bf16[32,32,384]{2,1,0:T(8,128)(2,1)S(1)} all-to-all(bf16[32,32,384]{2,1,0:T(8,128)(2,1)S(1)} %bitcast.10), channel_id=1, replica_groups=mesh['order'=32,'axial'=8] {'order'}, dimensions={0} | all-to-all | bytes 1572864 | tf_op jit(solution)/shard_map/all_to_all | solution.py:255
  85.6 2.4 %radial_analysis.1 = bf16[384,1024]{1,0:T(8,128)(2,1)S(1)} custom-call(bf16[1024,384]{1,0:T(8,128)(2,1)S(1)} %bitcast.9, s32[128,1]{1,0:T(8,128)S(1)} %reshape.29.lens_ref, bf16[128,128]{1,0:T(8,128)(2,1)S(1)} %copy-done.9, bf16[1024,1024]{1,0:T(8,128)(2,1)S(1)} %copy-done.3), custom_call_target="tpu_custom_call" | custom-call | tf_op jit(solution)/shard_map/radial_analysis/pallas_call | solution.py:236
  88.0 1.2 %reshape.28 = bf16[3,2,32,2,1024]{4,3,2,1,0:T(2,128)(2,1)} reshape(bf16[384,1024]{1,0:T(8,128)(2,1)S(1)} %radial_analysis.1) | data formatting | bytes 1572864 | tf_op jit(solution)/shard_map/reshape | solution.py:291
  (22 shorter events, 0.1 us)
Async XLA Ops:
  0.0 11.4 %copy-start.2 = (bf16[1024,1024]{1,0:T(8,128)(2,1)S(1)}, bf16[1024,1024]{1,0:T(8,128)(2,1)}, u32[]{:S(2)}) copy-start(bf16[1024,1024]{1,0:T(8,128)(2,1)} %constant.29.clone.table_ref) | copy-start | bytes 6291460
  0.0 9.6 %copy-start.10 = (s32[1024]{0:T(1024)S(1)}, s32[1024]{0:T(1024)}, u32[]{:S(2)}) copy-start(s32[1024]{0:T(1024)} %param.10) | copy-start | bytes 12292
  0.0 9.6 %copy-start.11 = (s32[1024]{0:T(1024)S(1)}, s32[1024]{0:T(1024)}, u32[]{:S(2)}) copy-start(s32[1024]{0:T(1024)} %param.11) | copy-start | bytes 12292
  3.1 18.9 %collective-permute-start.1 = (bf16[256,1024]{1,0:T(8,128)(2,1)S(1)}, bf16[256,1024]{1,0:T(8,128)(2,1)}, u32[]{:S(2)}, u32[]{:S(2)}) collective-permute-start(bf16[256,1024]{1,0:T(8,128)(2,1)S(1)} %slice.18.x_ref), channel_id=1, source_target_pairs={{0,7},{1,0},{2,1},{3,2},{4,3},{5,4},{6,5},{7,6},{8,15},{9,8},{10,9... | collective-permute-start | bytes 1572872 | tf_op jit(solution)/shard_map/ppermute | solution.py:251
  9.6 13.8 %collective-permute-start = (bf16[256,1024]{1,0:T(8,128)(2,1)S(1)}, bf16[256,1024]{1,0:T(8,128)(2,1)}, u32[]{:S(2)}, u32[]{:S(2)}) collective-permute-start(bf16[256,1024]{1,0:T(8,128)(2,1)S(1)} %slice.18.x_ref), channel_id=1, source_target_pairs={{0,1},{1,2},{2,3},{3,4},{4,5},{5,6},{6,7},{7,0},{8,9},{9,10},{10,1... | collective-permute-start | bytes 1572872 | tf_op jit(solution)/shard_map/ppermute | solution.py:251
  11.4 12.0 %copy-start.7 = (bf16[128,384]{1,0:T(8,128)(2,1)S(1)}, bf16[128,384]{1,0:T(8,128)(2,1)}, u32[]{:S(2)}) copy-start(bf16[128,384]{1,0:T(8,128)(2,1)} %constant.30.clone.rows_ref) | copy-start | bytes 294916
  13.1 0.8 copy-start.5
  13.9 19.7 %all-to-all-start = ((bf16[32,32,256]{2,1,0:T(8,128)(2,1)}), bf16[32,32,256]{2,1,0:T(8,128)(2,1)S(1)}, u32[]{:S(2)}, u32[]{:S(2)}) async-start(bf16[32,32,256]{2,1,0:T(8,128)(2,1)} %bitcast.12), calls=%async_computation | async-start | bytes 1048576 | tf_op jit(solution)/shard_map/all_to_all | solution.py:255
  26.4 0.8 copy-start.4
  33.5 19.1 %all-to-all-start.1 = ((bf16[32,32,256]{2,1,0:T(8,128)(2,1)}), bf16[32,32,256]{2,1,0:T(8,128)(2,1)S(1)}, u32[]{:S(2)}, u32[]{:S(2)}) async-start(bf16[32,32,256]{2,1,0:T(8,128)(2,1)} %bitcast.11), calls=%async_computation.1 | async-start | bytes 1048576 | tf_op jit(solution)/shard_map/all_to_all | solution.py:255
  37.3 15.4 %collective-permute-start.3 = (bf16[1024,128]{1,0:T(8,128)(2,1)S(1)}, bf16[1024,128]{1,0:T(8,128)(2,1)S(1)}, u32[]{:S(2)}, u32[]{:S(2)}) collective-permute-start(bf16[1024,128]{1,0:T(8,128)(2,1)S(1)} %slice.20), channel_id=1, source_target_pairs={{0,7},{1,0},{2,1},{3,2},{4,3},{5,4},{6,5},{7,6},{8,15},{9,8},{10,9... | collective-permute-start | bytes 786440 | tf_op jit(solution)/shard_map/ppermute | solution.py:251
  40.3 12.4 %collective-permute-start.2 = (bf16[1024,128]{1,0:T(8,128)(2,1)S(1)}, bf16[1024,128]{1,0:T(8,128)(2,1)S(1)}, u32[]{:S(2)}, u32[]{:S(2)}) collective-permute-start(bf16[1024,128]{1,0:T(8,128)(2,1)S(1)} %slice.20), channel_id=1, source_target_pairs={{0,1},{1,2},{2,3},{3,4},{4,5},{5,6},{6,7},{7,0},{8,9},{9,10},{10,1... | collective-permute-start | bytes 786440 | tf_op jit(solution)/shard_map/ppermute | solution.py:251
  40.5 12.2 %copy-start.6 = (bf16[384,256]{1,0:T(8,128)(2,1)S(1)}, bf16[384,256]{1,0:T(8,128)(2,1)}, u32[]{:S(2)}) copy-start(bf16[384,256]{1,0:T(8,128)(2,1)} %constant.32.clone.dz_ref) | copy-start | bytes 589828
  40.5 12.1 %copy-start.8 = (bf16[128,256]{1,0:T(8,128)(2,1)S(1)}, bf16[128,256]{1,0:T(8,128)(2,1)}, u32[]{:S(2)}) copy-start(bf16[128,256]{1,0:T(8,128)(2,1)} %constant.31.clone.both_ref) | copy-start | bytes 196612
  49.4 3.2 %copy-start = (bf16[2048,2048]{1,0:T(8,128)(2,1)}, bf16[2048,2048]{1,0:T(8,128)(2,1)S(1)}, u32[]{:S(2)}) copy-start(bf16[2048,2048]{1,0:T(8,128)(2,1)S(1)} %azimuthal_table.1.table_ref) | copy-start | bytes 25165828
  52.7 3.4 %copy-start.1 = (bf16[2048,2048]{1,0:T(8,128)(2,1)S(1)}, bf16[2048,2048]{1,0:T(8,128)(2,1)}, u32[]{:S(2)}) copy-start(bf16[2048,2048]{1,0:T(8,128)(2,1)} %copy-done) | copy-start | bytes 25165828
  56.1 29.5 %copy-start.3 = (bf16[1024,1024]{1,0:T(8,128)(2,1)S(1)}, bf16[1024,1024]{1,0:T(8,128)(2,1)}, u32[]{:S(2)}) copy-start(bf16[1024,1024]{1,0:T(8,128)(2,1)} %constant.34.clone.table_ref) | copy-start | bytes 6291460
  56.1 29.5 %copy-start.9 = (bf16[128,128]{1,0:T(8,128)(2,1)S(1)}, bf16[128,128]{1,0:T(8,128)(2,1)}, u32[]{:S(2)}) copy-start(bf16[128,128]{1,0:T(8,128)(2,1)} %constant.33.clone.back_ref) | copy-start | bytes 98308
where the time goes:
time: 89.6 us; the launch traced here: 89.2 us
  Pallas kernels  23.8 us (27%)
  blocking collectives  21.6 us (24%)
  starting transfers between devices  21.2 us (24%)
  local copies, waits for them, and re-layouts  14.3 us (16%)
  waiting for transfers between devices  7.72 us (9%)
    all_to_all x1, blocking collectives, exchange(): lax.all_to_all(block, 'order', split_axis=0, concat_axis=0, tiled=True)  21.6 us
    all_to_all x2, starting transfers between devices, exchange(): lax.all_to_all(block, 'order', split_axis=0, concat_axis=0, tiled=True)  11.7 us
    ppermute x4, starting transfers between devices, shift(): lax.ppermute(block, 'axial', [(i, (i + offset) % count) for i in range(co...  9.52 us
    pallas_call x1, Pallas kernels, azimuthal_table(): pl.pallas_call(table_kernel, grid=(groups,), out_shape=jax.ShapeDtypeStru...  8.87 us
    unnamed x24, local copies, waits for them, and re-layouts  8.26 us
    pallas_call x1, Pallas kernels, physical_stage(): pl.pallas_call(functools.partial(physical_kernel, groups, band, math.sqrt...  7.82 us
    all_to_all x2, waiting for transfers between devices, exchange(): lax.all_to_all(block, 'order', split_axis=0, concat_axis=0, tiled=True)  6.31 us
    slice x3, local copies, waits for them, and re-layouts, shards(): sloped, raw = (rows[:2 * width], rows[2 * width:])  4.31 us
  transfers between devices with their start and end apart: 6, of which 2 were waited for; matrix products, arithmetic and copies ran while one was open for 2% of the time, Pallas kernels for 15%

commit v1 on v0

--- a/solution.py
+++ b/solution.py
@@ -56,12 +56,17 @@
     return jnp.where(modes < lens, block.astype(F32) * weight, 0.0)
 
 
+def field_rows(ref, field):
+    block = ref[field]
+    return block.reshape(math.prod(block.shape[:-1]), block.shape[-1])
+
+
 def raw_kernel(x_ref, lens_ref, weight_ref, table_ref, out_ref, held):
     @pl.when(pl.program_id(0) == 0)
     def _():
-        for start in range(0, x_ref.shape[0], 128):
-            part = pl.ds(start, 128)
-            held[part, :] = masked_rows(x_ref[part, :], lens_ref[...], weight_ref[...]).astype(BF16)
+        for field in range(2):
+            rows = masked_rows(field_rows(x_ref, field), lens_ref[...], weight_ref[...])
+            held[field * rows.shape[0]:(field + 1) * rows.shape[0], :] = rows.astype(BF16)
 
     out_ref[...] = dot(table_ref[...], held[...], ((1,), (1,))).astype(BF16)
 
@@ -69,11 +74,14 @@
 def slope_kernel(x_ref, low_ref, high_ref, lens_ref, weight_ref, rows_ref, table_ref, out_ref, held):
     @pl.when(pl.program_id(0) == 0)
     def _():
-        for start in range(0, x_ref.shape[0], 128):
-            part = pl.ds(start, 128)
-            stacked = jnp.concatenate([x_ref[part, :], low_ref[part, :], high_ref[part, :]], axis=0)
+        for field in range(2):
+            stacked = jnp.concatenate(
+                [field_rows(x_ref, field), field_rows(low_ref, field), field_rows(high_ref, field)],
+                axis=0,
+            )
             slope = dot(rows_ref[...], stacked, ((1,), (0,)))
-            held[part, :] = masked_rows(slope, lens_ref[...], weight_ref[...]).astype(BF16)
+            rows = masked_rows(slope, lens_ref[...], weight_ref[...])
+            held[field * rows.shape[0]:(field + 1) * rows.shape[0], :] = rows.astype(BF16)
 
     out_ref[...] = dot(table_ref[...], held[...], ((1,), (1,))).astype(BF16)
 
@@ -82,33 +90,37 @@
     return pl.BlockSpec(shape, lambda i: (0,) * len(shape))
 
 
+def two_fields(shape, first):
+    return pl.BlockSpec((2,) + tuple(shape[1:]), lambda i: (first // 2,) + (0,) * (len(shape) - 1))
+
+
 def radial_raw(x, lens, weight, table, step=256):
-    rows, modes = x.shape
+    rows, modes = 2 * math.prod(x.shape[1:-1]), x.shape[-1]
     return pl.pallas_call(
         raw_kernel,
         grid=(R // step,),
-        out_shape=jax.ShapeDtypeStruct((R, rows), BF16),
-        in_specs=[whole(x.shape), whole(lens.shape), whole(weight.shape),
+        out_shape=pltpu.HBM((R, rows), BF16),
+        in_specs=[two_fields(x.shape, 2), whole(lens.shape), whole(weight.shape),
                   pl.BlockSpec((step, modes), lambda i: (i, 0))],
         out_specs=pl.BlockSpec((step, rows), lambda i: (i, 0)),
         scratch_shapes=[pltpu.VMEM((rows, modes), BF16)],
-        compiler_params=pltpu.CompilerParams(vmem_limit_bytes=24 << 20),
+        compiler_params=pltpu.CompilerParams(vmem_limit_bytes=16 << 20),
         name="radial_raw",
-    )(x, lens, weight, table)
+    )(in_hbm(x), lens, weight, in_hbm(table))
 
 
 def radial_slope(x, low, high, lens, weight, rows_map, table, step=256):
-    rows, modes = x.shape
+    rows, modes = 2 * math.prod(x.shape[1:-1]), x.shape[-1]
     return pl.pallas_call(
         slope_kernel,
         grid=(R // step,),
-        out_shape=jax.ShapeDtypeStruct((R, rows), BF16),
-        in_specs=[whole(x.shape), whole(x.shape), whole(x.shape), whole(lens.shape),
+        out_shape=pltpu.HBM((R, rows), BF16),
+        in_specs=[two_fields(x.shape, 0), whole(low.shape), whole(high.shape), whole(lens.shape),
                   whole(weight.shape), whole(rows_map.shape),
                   pl.BlockSpec((step, modes), lambda i: (i, 0))],
         out_specs=pl.BlockSpec((step, rows), lambda i: (i, 0)),
         scratch_shapes=[pltpu.VMEM((rows, modes), BF16)],
-        compiler_params=pltpu.CompilerParams(vmem_limit_bytes=24 << 20),
+        compiler_params=pltpu.CompilerParams(vmem_limit_bytes=16 << 20),
         name="radial_slope",
     )(x, low, high, lens, weight, rows_map, table)
 
@@ -137,50 +149,86 @@
     return pl.pallas_call(
         table_kernel,
         grid=(groups,),
-        out_shape=jax.ShapeDtypeStruct((groups * 2 * slots, points), BF16),
+        out_shape=pltpu.HBM((groups * 2 * slots, points), BF16),
         in_specs=[pl.BlockSpec((slots, 1), lambda i: (i, 0))],
         out_specs=pl.BlockSpec((2 * slots, points), lambda i: (i, 0)),
-        compiler_params=pltpu.CompilerParams(vmem_limit_bytes=24 << 20),
+        compiler_params=pltpu.CompilerParams(vmem_limit_bytes=8 << 20),
         name="azimuthal_table",
     )(orders)
 
 
-def physical_kernel(groups, band, scale, raw_ref, slope_ref, low_ref, high_ref, both_ref,
-                    dz_ref, table_ref, out_ref, lhs, acc):
+def place_field(lhs, mapped, row, groups, band):
+    width = mapped.shape[1] // 2
+    low_lanes = lax.broadcasted_iota(jnp.int32, (band, width), 1) < width // 2
+    for pair in range(groups // 2):
+        even = mapped[2 * pair * band:(2 * pair + 1) * band]
+        odd = mapped[(2 * pair + 1) * band:(2 * pair + 2) * band]
+        first = jnp.where(low_lanes, even[:, :width], odd[:, width:])
+        second = jnp.where(low_lanes, even[:, width:], odd[:, :width])
+        cols = pl.ds(pair * width, width)
+        lhs[row:row + band, cols] = first.astype(BF16)
+        lhs[row + band:row + 2 * band, cols] = second.astype(BF16)
+
+
+def axial_kernel(groups, band, raw_ref, low_ref, high_ref, both_ref, dz_ref, table_ref,
+                 axial_ref, product_ref, lhs):
+    width = both_ref.shape[0]
+
+    @pl.when(pl.program_id(0) == 0)
+    def _():
+        joined = jnp.concatenate([raw_ref[:, 0:width], low_ref[...], high_ref[...]], axis=1)
+        place_field(lhs, dot(joined, dz_ref[...], ((1,), (0,))), 0, groups, band)
+        mapped = dot(raw_ref[:, width:2 * width], both_ref[...], ((1,), (0,)))
+        place_field(lhs, mapped, 2 * band, groups, band)
+
+    values = dot(lhs[...], table_ref[...], ((1,), (0,)))
+    axial = values[2 * band:] * (1.0 / 12.0)
+    axial_ref[...] = axial
+    product_ref[...] = (values[:2 * band] * axial).astype(BF16)
+
+
+def axial_stage(raw, low, high, both, dz, table, groups, band, step=512):
+    rows, points = table.shape
+    columns = pl.BlockSpec((2 * band, step), lambda i: (0, i))
+    return pl.pallas_call(
+        functools.partial(axial_kernel, groups, band),
+        grid=(points // step,),
+        out_shape=(jax.ShapeDtypeStruct((2 * band, points), F32),
+                   jax.ShapeDtypeStruct((2 * band, points), BF16)),
+        in_specs=[whole(raw.shape), whole(low.shape), whole(high.shape),
+                  whole(both.shape), whole(dz.shape),
+                  pl.BlockSpec((rows, step), lambda i: (0, i))],
+        out_specs=(columns, columns),
+        scratch_shapes=[pltpu.VMEM((4 * band, rows), BF16)],
+        compiler_params=pltpu.CompilerParams(vmem_limit_bytes=20 << 20),
+        name="axial_stage",
+    )(raw, low, high, both, dz, in_hbm(table))
+
+
+def physical_kernel(groups, band, scale, slope_ref, axial_ref, product_ref, both_ref,
+                    table_ref, out_ref, lhs, acc):
     step = pl.program_id(0)
     width = both_ref.shape[0]
     half = width // 2
-    low_lanes = lax.broadcasted_iota(jnp.int32, (band, width), 1) < half
 
     @pl.when(step == 0)
     def _():
         acc[...] = jnp.zeros_like(acc)
-        for field in range(4):
-            if field < 2:
-                mapped = dot(slope_ref[:, field * width:(field + 1) * width], both_ref[...], ((1,), (0,)))
-            elif field == 2:
-                joined = jnp.concatenate([raw_ref[:, 0:width], low_ref[...], high_ref[...]], axis=1)
-                mapped = dot(joined, dz_ref[...], ((1,), (0,)))
-            else:
-                mapped = dot(raw_ref[:, width:2 * width], both_ref[...], ((1,), (0,)))
-            for pair in range(groups // 2):
-                even = mapped[2 * pair * band:(2 * pair + 1) * band]
-                odd = mapped[(2 * pair + 1) * band:(2 * pair + 2) * band]
-                first = jnp.where(low_lanes, even[:, :width], odd[:, width:])
-                second = jnp.where(low_lanes, even[:, width:], odd[:, :width])
-                cols = pl.ds(pair * width, width)
-                lhs[(2 * field) * band:(2 * field + 1) * band, cols] = first.astype(BF16)
-                lhs[(2 * field + 1) * band:(2 * field + 2) * band, cols] = second.astype(BF16)
+        for field in range(2):
+            mapped = dot(slope_ref[:, field * width:(field + 1) * width], both_ref[...], ((1,), (0,)))
+            place_field(lhs, mapped, 2 * field * band, groups, band)
 
     values = dot(lhs[...], table_ref[...], ((1,), (0,)))
-    axial = values[6 * band:8 * band] * (1.0 / 12.0)
+    axial = axial_ref[...]
     products = jnp.concatenate(
-        [(values[2 * g * band:(2 * g + 2) * band] * axial).astype(BF16) for g in range(3)], axis=0
+        [(values[:2 * band] * axial).astype(BF16), (values[2 * band:] * axial).astype(BF16),
+         product_ref[...]], axis=0
     )
     acc[...] += dot(products, table_ref[...], ((1,), (1,)))
 
     @pl.when(step == pl.num_programs(0) - 1)
     def _():
+        low_lanes = lax.broadcasted_iota(jnp.int32, (band, width), 1) < half
         for g in range(3):
             for pair in range(groups // 2):
                 cols = pl.ds(pair * width, width)
@@ -193,21 +241,21 @@
                 out_ref[(2 * pair + 1) * band:(2 * pair + 2) * band, out_cols] = odd.astype(BF16)
 
 
-def physical_stage(raw, slope, low, high, both, dz, table, groups, band, step=512):
+def physical_stage(slope, axial, product, both, table, groups, band, step=512):
     rows, points = table.shape
     width = both.shape[0]
+    columns = pl.BlockSpec((2 * band, step), lambda i: (0, i))
     return pl.pallas_call(
         functools.partial(physical_kernel, groups, band, math.sqrt(2.0 / points)),
         grid=(points // step,),
         out_shape=jax.ShapeDtypeStruct((groups * band, 3 * width), BF16),
-        in_specs=[whole(raw.shape), whole(slope.shape), whole(low.shape), whole(high.shape),
-                  whole(both.shape), whole(dz.shape),
+        in_specs=[whole(slope.shape), columns, columns, whole(both.shape),
                   pl.BlockSpec((rows, step), lambda i: (0, i))],
         out_specs=whole((groups * band, 3 * width)),
-        scratch_shapes=[pltpu.VMEM((8 * band, rows), BF16), pltpu.VMEM((6 * band, rows), F32)],
-        compiler_params=pltpu.CompilerParams(vmem_limit_bytes=40 << 20),
+        scratch_shapes=[pltpu.VMEM((4 * band, rows), BF16), pltpu.VMEM((6 * band, rows), F32)],
+        compiler_params=pltpu.CompilerParams(vmem_limit_bytes=24 << 20),
         name="physical_stage",
-    )(raw, slope, low, high, both, dz, table)
+    )(slope, axial, product, both, in_hbm(table))
 
 
 def final_kernel(x_ref, lens_ref, back_ref, table_ref, out_ref, held):
@@ -225,25 +273,28 @@
     modes = lax.broadcasted_iota(jnp.int32, (width, columns), 1) + step * columns
     keep = modes < lens_ref[...]
     for g in range(3):
-        out_ref[g * width:(g + 1) * width, :] = jnp.where(
-            keep, result[g * width:(g + 1) * width], 0.0
-        ).astype(BF16)
-
-
-def radial_analysis(x, lens, back, table, step=256):
+        rows = jnp.where(keep, result[g * width:(g + 1) * width], 0.0).astype(BF16)
+        out_ref[g] = rows.reshape(out_ref.shape[1:])
+
+
+def radial_analysis(x, lens, back, table, shape, step=256):
     radii, lanes = x.shape
     modes = table.shape[1]
     return pl.pallas_call(
         final_kernel,
         grid=(modes // step,),
-        out_shape=jax.ShapeDtypeStruct((lanes, modes), BF16),
+        out_shape=pltpu.HBM(shape, BF16),
         in_specs=[whole(x.shape), whole(lens.shape), whole(back.shape),
                   pl.BlockSpec((radii, step), lambda i: (0, i))],
-        out_specs=pl.BlockSpec((lanes, step), lambda i: (0, i)),
+        out_specs=pl.BlockSpec(tuple(shape[:-1]) + (step,), lambda i: (0, 0, 0, 0, i)),
         scratch_shapes=[pltpu.VMEM((radii, lanes), BF16)],
-        compiler_params=pltpu.CompilerParams(vmem_limit_bytes=24 << 20),
+        compiler_params=pltpu.CompilerParams(vmem_limit_bytes=16 << 20),
         name="radial_analysis",
     )(x, lens, back, table)
+
+
+def in_hbm(x):
+    return pltpu.with_memory_space_constraint(x, pltpu.HBM)
 
 
 def shift(block, offset):
@@ -265,8 +316,7 @@
     synthesis, analysis = radial_constants(R, modes)
     rows_map, both, dz, back = plane_matrices(slots)
 
-    rows = coefficients.reshape(field_count * width, modes)
-    sloped, raw = rows[:2 * width], rows[2 * width:]
+    sloped = coefficients[:2]
     low, high = shift(sloped, 1), shift(sloped, -1)
 
     owned = lax.dynamic_slice_in_dim(order_lists, lax.axis_index("order") * slots, slots)
@@ -279,16 +329,18 @@
     weight = jnp.where(owned == 0, 1.0, 2.0).astype(F32)
     weight = jnp.broadcast_to(weight[None, :, None], spread).reshape(width, 1)
 
-    raw_bands = exchange(radial_raw(raw, lens, weight, synthesis))
+    raw_bands = exchange(radial_raw(coefficients, lens, weight, synthesis))
     table = azimuthal_table(order_lists.reshape(order_count, 1), groups, slots, points)
     own_band = raw_bands[:, :width]
     low_band, high_band = shift(own_band, 1), shift(own_band, -1)
-    slope_bands = exchange(radial_slope(sloped, low, high, lens, weight, rows_map, synthesis))
-    spectral = physical_stage(
-        raw_bands, slope_bands, low_band, high_band, both, dz, table, groups, band
-    )
-    result = radial_analysis(exchange(spectral), lens, back, analysis)
-    return result.reshape(3, part_count, slots, planes, modes)
+    later_lens, table = lax.optimization_barrier((lens, table))
+    slope_bands = exchange(
+        radial_slope(coefficients, low, high, later_lens, weight, rows_map, synthesis)
+    )
+    axial, product = axial_stage(raw_bands, low_band, high_band, both, dz, table, groups, band)
+    spectral = physical_stage(slope_bands, axial, product, both, table, groups, band)
+    shape = (3, part_count, slots, planes, modes)
+    return radial_analysis(exchange(spectral), lens, back, analysis, shape)
 
 
 def solution(mesh):

time: 89.6 us -> 104 us (1.16)
  Pallas kernels: 23.8 us -> 41.4 us
  local copies, waits for them, and re-layouts: 14.3 us -> 6.78 us
  starting transfers between devices: 21.2 us -> 24.6 us
  waiting for transfers between devices: 7.72 us -> 6.22 us
  other arithmetic: 0.26 us -> 1.64 us
    pallas_call x4 -> x5, Pallas kernels: 16 us -> 33.6 us  [the longest x1 16 us: azimuthal_table(): pl.pallas_call(table_kernel, grid=(groups,), out_shape=pltpu.HBM((groups...]
    all_to_all x2, waiting for transfers between devices: 6.31 us -> 0.01 us  [exchange(): lax.all_to_all(block, 'order', split_axis=0, concat_axis=0, tiled=True)]
    unnamed x24 -> x18, local copies, waits for them, and re-layouts: 8.26 us -> 2 us
    ppermute x4, waiting for transfers between devices: 1.42 us -> 6.21 us  [shift(): lax.ppermute(block, 'axial', [(i, (i + offset) % count) for i in range(co...]
    all_to_all x2, starting transfers between devices: 11.7 us -> 15.5 us  [exchange(): lax.all_to_all(block, 'order', split_axis=0, concat_axis=0, tiled=True)]
    slice x3 -> x1, local copies, waits for them, and re-layouts: 4.31 us -> 2.19 us  [shards(): sloped = coefficients[:2]]
    reshape x1 -> x0, local copies, waits for them, and re-layouts: 1.18 us -> none  [shards(): return result.reshape(3, part_count, slots, planes, modes)]
  transfers between devices with their start and end apart: 6 -> 6, of which waited for: 2 -> 1; matrix products, arithmetic and copies ran while one was open for 2% -> 4% of each run, Pallas kernels for 15% -> 29%
where the time goes in v1:
time: 104 us; the launch traced here: 103 us
  Pallas kernels  41.4 us (40%)
  starting transfers between devices  24.6 us (24%)
  blocking collectives  22.1 us (21%)
  local copies, waits for them, and re-layouts  6.78 us (7%)
  waiting for transfers between devices  6.22 us (6%)
  other arithmetic  1.64 us (2%)
    all_to_all x1, blocking collectives, exchange(): lax.all_to_all(block, 'order', split_axis=0, concat_axis=0, tiled=True)  22.1 us
    pallas_call x1, Pallas kernels, azimuthal_table(): pl.pallas_call(table_kernel, grid=(groups,), out_shape=pltpu.HBM((groups...  16 us
    all_to_all x2, starting transfers between devices, exchange(): lax.all_to_all(block, 'order', split_axis=0, concat_axis=0, tiled=True)  15.5 us
    ppermute x4, starting transfers between devices, shift(): lax.ppermute(block, 'axial', [(i, (i + offset) % count) for i in range(co...  9.16 us
    pallas_call x1, Pallas kernels, physical_stage(): pl.pallas_call(functools.partial(physical_kernel, groups, band, math.sqrt...  7.86 us
    ppermute x4, waiting for transfers between devices, shift(): lax.ppermute(block, 'axial', [(i, (i + offset) % count) for i in range(co...  6.21 us
    pallas_call x1, Pallas kernels, axial_stage(): pl.pallas_call(functools.partial(axial_kernel, groups, band), grid=(point...  5.59 us
    pallas_call x1, Pallas kernels, radial_raw(): pl.pallas_call(raw_kernel, grid=(R // step,), out_shape=pltpu.HBM((R, row...  4.68 us
  transfers between devices with their start and end apart: 6, of which 1 were waited for; matrix products, arithmetic and copies ran while one was open for 4% of the time, Pallas kernels for 29%

profile of v1, /device:TPU:1, one launch (start us, length us, event | category | flops | bytes accessed | tf_op | source)
XLA Modules:
  0.0 102.9 jit_solution(13816454469854212940)
XLA Ops:
  0.0 2.2 %slice.6 = bf16[2,2,32,2,1024]{4,3,2,1,0:T(2,128)(2,1)} slice(bf16[4,2,32,2,1024]{4,3,2,1,0:T(2,128)(2,1)} %x_ref.3), slice={[0:2], [0:2], [0:32], [0:2], [0:1024]} | slice | bytes 1048576 | tf_op jit(solution)/shard_map/slice | solution.py:319
  2.2 2.5 %collective-permute-start = (bf16[2,2,32,2,1024]{4,3,2,1,0:T(2,128)(2,1)}, bf16[2,2,32,2,1024]{4,3,2,1,0:T(2,128)(2,1)}, u32[]{:S(2)}, u32[]{:S(2)}) collective-permute-start(bf16[2,2,32,2,1024]{4,3,2,1,0:T(2,128)(2,1)} %slice.6), channel_id=1, source_target_pairs={{0,1},{1,2},{2,3},{3,4},{4,5},{5,6},{6,7},{7,0},{8,9},{9,10},{10,1... | collective-permute-start | bytes 1572872 | tf_op jit(solution)/shard_map/ppermute | solution.py:302
  4.7 3.9 %collective-permute-start.1 = (bf16[2,2,32,2,1024]{4,3,2,1,0:T(2,128)(2,1)}, bf16[2,2,32,2,1024]{4,3,2,1,0:T(2,128)(2,1)}, u32[]{:S(2)}, u32[]{:S(2)}) collective-permute-start(bf16[2,2,32,2,1024]{4,3,2,1,0:T(2,128)(2,1)} %slice.6), channel_id=1, source_target_pairs={{0,7},{1,0},{2,1},{3,2},{4,3},{5,4},{6,5},{7,6},{8,15},{9,8},{10,9... | collective-permute-start | bytes 1572872 | tf_op jit(solution)/shard_map/ppermute | solution.py:302
  8.6 0.8 compare_select_fusion
  9.4 0.9 select_reduce_fusion
  10.2 0.1 broadcast_in_dim.37
  10.3 0.1 reshape.19
  10.5 0.1 broadcast_in_dim.40
  10.5 0.1 reshape.22.weight_ref
  10.6 0.1 copy.24.lens_ref
  10.7 0.0 copy-start.8
  10.7 4.7 %radial_raw.1 = bf16[1024,256]{1,0:T(8,128)(2,1)} custom-call(bf16[4,2,32,2,1024]{4,3,2,1,0:T(2,128)(2,1)} %x_ref.3, s32[128,1]{1,0:T(8,128)S(1)} %copy.24.lens_ref, f32[128,1]{1,0:T(8,128)S(1)} %reshape.22.weight_ref, bf16[1024,1024]{1,0:T(8,128)(2,1)} %constant.29.clone.table_ref), custom_call_target="tpu_custom_call" | custom-call | tf_op jit(solution)/shard_map/radial_raw/pallas_call | solution.py:99
  15.4 8.1 %all-to-all-start.1 = ((bf16[32,32,256]{2,1,0:T(8,128)(2,1)}), bf16[32,32,256]{2,1,0:T(8,128)(2,1)}, u32[]{:S(2)}, u32[]{:S(2)}) async-start(bf16[32,32,256]{2,1,0:T(8,128)(2,1)} %bitcast.11), calls=%async_computation.1 | async-start | bytes 1048576 | tf_op jit(solution)/shard_map/all_to_all | solution.py:306
  23.5 1.0 copy.21.orders_ref
  24.6 1.0 %copy-done.3 = s32[1024,1]{1,0:T(8,128)S(1)} copy-done((s32[1024,1]{1,0:T(8,128)S(1)}, s32[1024,1]{1,0:T(8,128)}, u32[]{:S(2)}) %copy-start.3) | copy-done | bytes 4120
  25.6 16.0 %azimuthal_table.1.table_ref = bf16[2048,2048]{1,0:T(8,128)(2,1)} custom-call(s32[1024,1]{1,0:T(8,128)S(1)} %copy-done.3), custom_call_target="tpu_custom_call" | custom-call | tf_op jit(solution)/shard_map/azimuthal_table/pallas_call | solution.py:149
  41.6 0.1 copy.22.lens_ref
  41.7 0.0 collective-permute-done.low_ref
  41.8 0.0 collective-permute-done.1.high_ref
  41.8 4.0 %radial_slope.1 = bf16[1024,256]{1,0:T(8,128)(2,1)} custom-call(bf16[4,2,32,2,1024]{4,3,2,1,0:T(2,128)(2,1)S(1)} %copy-done.1, bf16[2,2,32,2,1024]{4,3,2,1,0:T(2,128)(2,1)} %collective-permute-done.low_ref, bf16[2,2,32,2,1024]{4,3,2,1,0:T(2,128)(2,1)} %collective-permute-done.1.high_ref, s32[128,1]{1,0:T(8,128)S(1)} %copy.22.lens_ref, ...), custom_call_target="tpu_custom_call" | custom-call | tf_op jit(solution)/shard_map/radial_slope/pallas_call | solution.py:114
  45.8 7.4 %all-to-all-start = ((bf16[32,32,256]{2,1,0:T(8,128)(2,1)}), bf16[32,32,256]{2,1,0:T(8,128)(2,1)S(1)}, u32[]{:S(2)}, u32[]{:S(2)}) async-start(bf16[32,32,256]{2,1,0:T(8,128)(2,1)} %bitcast.10), calls=%async_computation | async-start | bytes 1048576 | tf_op jit(solution)/shard_map/all_to_all | solution.py:306
  53.2 1.0 slice.8
  54.2 0.1 collective-permute-start.2
  54.3 2.7 %collective-permute-start.3 = (bf16[1024,128]{1,0:T(8,128)(2,1)S(1)}, bf16[1024,128]{1,0:T(8,128)(2,1)S(1)}, u32[]{:S(2)}, u32[]{:S(2)}) collective-permute-start(bf16[1024,128]{1,0:T(8,128)(2,1)S(1)} %slice.8), channel_id=1, source_target_pairs={{0,7},{1,0},{2,1},{3,2},{4,3},{5,4},{6,5},{7,6},{8,15},{9,8},{10,9... | collective-permute-start | bytes 786440 | tf_op jit(solution)/shard_map/ppermute | solution.py:302
  57.0 6.2 %collective-permute-done.2.low_ref = bf16[1024,128]{1,0:T(8,128)(2,1)S(1)} collective-permute-done((bf16[1024,128]{1,0:T(8,128)(2,1)S(1)}, bf16[1024,128]{1,0:T(8,128)(2,1)S(1)}, u32[]{:S(2)}, u32[]{:S(2)}) %collective-permute-start.2) | collective-permute-done | bytes 262176 | tf_op jit(solution)/shard_map/ppermute | solution.py:302
  63.2 0.9 copy-done.5
  64.1 5.6 %axial_stage.1 = (f32[64,2048]{1,0:T(8,128)S(1)}, bf16[64,2048]{1,0:T(8,128)(2,1)S(1)}) custom-call(bf16[1024,256]{1,0:T(8,128)(2,1)} %bitcast.4.raw_ref, bf16[1024,128]{1,0:T(8,128)(2,1)S(1)} %collective-permute-done.2.low_ref, bf16[1024,128]{1,0:T(8,128)(2,1)S(1)} %collective-permute-done.3.high_ref, bf16[128,256]{1,0:T(8,128)(2,1)S(1)} %copy-done.4, ...), custom_call_target="tpu_custom_call" | custom-call | tf_op jit(solution)/shard_map/axial_stage/pallas_call | solution.py:193
  69.7 0.0 copy-start.2
  69.7 0.0 copy-start.7
  69.7 7.9 %physical_stage.1 = bf16[1024,384]{1,0:T(8,128)(2,1)S(1)} custom-call(bf16[1024,256]{1,0:T(8,128)(2,1)S(1)} %bitcast.9, f32[64,2048]{1,0:T(8,128)S(1)} %get-tuple-element.11.axial_ref, bf16[64,2048]{1,0:T(8,128)(2,1)S(1)} %get-tuple-element.12.product_ref, bf16[128,256]{1,0:T(8,128)(2,1)S(1)} %copy-done.4, bf16[2048,2048]{1,0:T(8,128)(2,1)} %azimuthal_table.1.table_ref), custom_call_target="tpu_custom_call" | custom-call | tf_op jit(solution)/shard_map/physical_stage/pallas_call | solution.py:248
  77.6 22.1 %all_to_all.33 = bf16[32,32,384]{2,1,0:T(8,128)(2,1)S(1)} all-to-all(bf16[32,32,384]{2,1,0:T(8,128)(2,1)S(1)} %bitcast.7), channel_id=1, replica_groups=mesh['order'=32,'axial'=8] {'order'}, dimensions={0} | all-to-all | bytes 1572864 | tf_op jit(solution)/shard_map/all_to_all | solution.py:306
  99.7 3.2 %radial_analysis.1 = bf16[3,2,32,2,1024]{4,3,2,1,0:T(2,128)(2,1)} custom-call(bf16[1024,384]{1,0:T(8,128)(2,1)S(1)} %bitcast.8, s32[128,1]{1,0:T(8,128)S(1)} %copy.24.lens_ref, bf16[128,128]{1,0:T(8,128)(2,1)S(1)} %copy-done.7, bf16[1024,1024]{1,0:T(8,128)(2,1)S(1)} %copy-done.2), custom_call_target="tpu_custom_call" | custom-call | tf_op jit(solution)/shard_map/radial_analysis/pallas_call | solution.py:283
  (16 shorter events, 0.0 us)
Async XLA Ops:
  2.2 39.5 %collective-permute-start = (bf16[2,2,32,2,1024]{4,3,2,1,0:T(2,128)(2,1)}, bf16[2,2,32,2,1024]{4,3,2,1,0:T(2,128)(2,1)}, u32[]{:S(2)}, u32[]{:S(2)}) collective-permute-start(bf16[2,2,32,2,1024]{4,3,2,1,0:T(2,128)(2,1)} %slice.6), channel_id=1, source_target_pairs={{0,1},{1,2},{2,3},{3,4},{4,5},{5,6},{6,7},{7,0},{8,9},{9,10},{10,1... | collective-permute-start | bytes 1572872 | tf_op jit(solution)/shard_map/ppermute | solution.py:302
  4.7 37.1 %collective-permute-start.1 = (bf16[2,2,32,2,1024]{4,3,2,1,0:T(2,128)(2,1)}, bf16[2,2,32,2,1024]{4,3,2,1,0:T(2,128)(2,1)}, u32[]{:S(2)}, u32[]{:S(2)}) collective-permute-start(bf16[2,2,32,2,1024]{4,3,2,1,0:T(2,128)(2,1)} %slice.6), channel_id=1, source_target_pairs={{0,7},{1,0},{2,1},{3,2},{4,3},{5,4},{6,5},{7,6},{8,15},{9,8},{10,9... | collective-permute-start | bytes 1572872 | tf_op jit(solution)/shard_map/ppermute | solution.py:302
  10.7 12.8 %copy-start.8 = (s32[1024]{0:T(1024)S(1)}, s32[1024]{0:T(1024)}, u32[]{:S(2)}) copy-start(s32[1024]{0:T(1024)} %param.10) | copy-start | bytes 12292
  15.4 30.4 %all-to-all-start.1 = ((bf16[32,32,256]{2,1,0:T(8,128)(2,1)}), bf16[32,32,256]{2,1,0:T(8,128)(2,1)}, u32[]{:S(2)}, u32[]{:S(2)}) async-start(bf16[32,32,256]{2,1,0:T(8,128)(2,1)} %bitcast.11), calls=%async_computation.1 | async-start | bytes 1048576 | tf_op jit(solution)/shard_map/all_to_all | solution.py:306
  24.6 1.0 %copy-start.3 = (s32[1024,1]{1,0:T(8,128)S(1)}, s32[1024,1]{1,0:T(8,128)}, u32[]{:S(2)}) copy-start(s32[1024,1]{1,0:T(8,128)} %copy.21.orders_ref) | copy-start | bytes 12292
  25.6 16.2 %copy-start = (bf16[1024,1024]{1,0:T(8,128)(2,1)S(1)}, bf16[1024,1024]{1,0:T(8,128)(2,1)}, u32[]{:S(2)}) copy-start(bf16[1024,1024]{1,0:T(8,128)(2,1)} %constant.29.clone.table_ref) | copy-start | bytes 6291460
  25.6 16.2 %copy-start.1 = (bf16[4,2,32,2,1024]{4,3,2,1,0:T(2,128)(2,1)S(1)}, bf16[4,2,32,2,1024]{4,3,2,1,0:T(2,128)(2,1)}, u32[]{:S(2)}) copy-start(bf16[4,2,32,2,1024]{4,3,2,1,0:T(2,128)(2,1)} %x_ref.3) | copy-start | bytes 3145732
  25.6 16.2 %copy-start.6 = (bf16[128,384]{1,0:T(8,128)(2,1)S(1)}, bf16[128,384]{1,0:T(8,128)(2,1)}, u32[]{:S(2)}) copy-start(bf16[128,384]{1,0:T(8,128)(2,1)} %constant.30.clone.rows_ref) | copy-start | bytes 294916
  41.7 21.4 %copy-start.4 = (bf16[128,256]{1,0:T(8,128)(2,1)S(1)}, bf16[128,256]{1,0:T(8,128)(2,1)}, u32[]{:S(2)}) copy-start(bf16[128,256]{1,0:T(8,128)(2,1)} %constant.31.clone.both_ref) | copy-start | bytes 196612
  45.8 23.9 %all-to-all-start = ((bf16[32,32,256]{2,1,0:T(8,128)(2,1)}), bf16[32,32,256]{2,1,0:T(8,128)(2,1)S(1)}, u32[]{:S(2)}, u32[]{:S(2)}) async-start(bf16[32,32,256]{2,1,0:T(8,128)(2,1)} %bitcast.10), calls=%async_computation | async-start | bytes 1048576 | tf_op jit(solution)/shard_map/all_to_all | solution.py:306
  54.2 9.0 %collective-permute-start.2 = (bf16[1024,128]{1,0:T(8,128)(2,1)S(1)}, bf16[1024,128]{1,0:T(8,128)(2,1)S(1)}, u32[]{:S(2)}, u32[]{:S(2)}) collective-permute-start(bf16[1024,128]{1,0:T(8,128)(2,1)S(1)} %slice.8), channel_id=1, source_target_pairs={{0,1},{1,2},{2,3},{3,4},{4,5},{5,6},{6,7},{7,0},{8,9},{9,10},{10,1... | collective-permute-start | bytes 786440 | tf_op jit(solution)/shard_map/ppermute | solution.py:302
  54.3 8.9 %collective-permute-start.3 = (bf16[1024,128]{1,0:T(8,128)(2,1)S(1)}, bf16[1024,128]{1,0:T(8,128)(2,1)S(1)}, u32[]{:S(2)}, u32[]{:S(2)}) collective-permute-start(bf16[1024,128]{1,0:T(8,128)(2,1)S(1)} %slice.8), channel_id=1, source_target_pairs={{0,7},{1,0},{2,1},{3,2},{4,3},{5,4},{6,5},{7,6},{8,15},{9,8},{10,9... | collective-permute-start | bytes 786440 | tf_op jit(solution)/shard_map/ppermute | solution.py:302
  63.2 0.9 copy-start.5
  69.7 30.0 %copy-start.2 = (bf16[1024,1024]{1,0:T(8,128)(2,1)S(1)}, bf16[1024,1024]{1,0:T(8,128)(2,1)}, u32[]{:S(2)}) copy-start(bf16[1024,1024]{1,0:T(8,128)(2,1)} %constant.34.clone.table_ref) | copy-start | bytes 6291460
  69.7 30.0 %copy-start.7 = (bf16[128,128]{1,0:T(8,128)(2,1)S(1)}, bf16[128,128]{1,0:T(8,128)(2,1)}, u32[]{:S(2)}) copy-start(bf16[128,128]{1,0:T(8,128)(2,1)} %constant.33.clone.back_ref) | copy-start | bytes 98308
